TPU v7x, 32 devices: a whole 2x2x4 slice. The times are simulated.
32 devices in a mesh: pages: 2 (over y), tile: 4 (over z), mp: 2 (over x), batch: 2 (over core).
Axes of the slice: x: 2, y: 2, z: 4, core: 2. Of those that a mesh axis runs over, the one named last changes fastest.
Arguments:
- page_cells: bfloat16 [4, 48, 24, 1024], P(('pages', 'batch'), 'tile'), parts along dimension 0, may hold values from -40 to 40
- text_states: bfloat16 [4, 1024, 1024], P(('pages', 'batch'), 'tile'), parts along dimension 0, may hold values from -40 to 40
- enc_query: bfloat16 [1024, 1024], P('batch', 'mp'), may hold values from -2.5 to 2.5
- enc_keyval: bfloat16 [1024, 2, 1024], P('batch', None, 'mp'), may hold values from -0.1875 to 0.1875
- enc_proj: bfloat16 [1024, 1024], P('mp', 'batch'), may hold values from -0.1875 to 0.1875
- dec_query: bfloat16 [1024, 1024], P('batch', 'mp'), may hold values from -2.5 to 2.5
- dec_keyval: bfloat16 [1024, 2, 1024], P('batch', None, 'mp'), may hold values from -0.1875 to 0.1875
- dec_out: bfloat16 [1024, 1024], P('mp', 'batch'), may hold values from -0.1875 to 0.1875
Outputs:
- encoded: bfloat16 [4, 48, 24, 1024], P(('pages', 'batch'), 'tile'), parts along dimension 0
- decoded: bfloat16 [4, 1024, 1024], P(('pages', 'batch'), ('tile', 'mp')), parts along dimension 0
There are 2 independent parts, one for each index of `pages`. A program takes and returns all parts, laid end to end along the dimension named above; an argument that names none is the same for every part. Nothing has to cross between parts.
All inputs are finite; a program needn't handle non-finite values.
Results may differ from a plain program's by a relative error of at most 0.012.
Values may be sent and summed in bfloat16 or wider, within the bound.
No kernel may reach another device: no remote copies, remote signals or barrier semaphores. Data moves between devices by JAX's collectives and lax.ppermute only.
A program may use at most 64 MiB of HBM per device.

v0:
```python
import math
import jax
import jax.numpy as jnp
from jax import lax
from jax.sharding import PartitionSpec as P

HEAD_ENC = 32
HEAD_DEC = 64


def from_behind(value, axis, by):
    devices = lax.axis_size(axis)
    return lax.ppermute(value, axis, [(i, (i + by) % devices) for i in range(devices)])


def layer_norm(values):
    center = values - jnp.mean(values, axis=-1, keepdims=True)
    variance = jnp.mean(center * center, axis=-1, keepdims=True)
    return center / jnp.sqrt(variance + 1e-05)


def regions(length, window, offset):
    index_row = jnp.arange(length, dtype=jnp.int32)
    return jnp.where(
        index_row < length - window, 0, jnp.where(index_row < length - offset, 1, 2)
    ).astype(jnp.int32)


def body(page_cells, text_states, enc_query, enc_keyval, enc_proj, dec_query, dec_keyval, dec_out):
    wq_enc, wkv_enc, wproj_enc, wq_dec, wkv_dec, wout_dec = (
        lax.all_gather(enc_query, "batch", axis=0, tiled=True),
        lax.all_gather(enc_keyval, "batch", axis=0, tiled=True),
        lax.all_gather(enc_proj, "batch", axis=1, tiled=True),
        lax.all_gather(dec_query, "batch", axis=0, tiled=True),
        lax.all_gather(dec_keyval, "batch", axis=0, tiled=True),
        lax.all_gather(dec_out, "batch", axis=1, tiled=True),
    )
    pages_here, window, columns, width = page_cells.shape
    offset = window // 2
    own_rows = window * columns
    hq_enc = wq_enc.shape[1]
    heads_enc = hq_enc // HEAD_ENC
    joined = jnp.concatenate([wq_enc, wkv_enc.reshape(width, 2 * hq_enc)], axis=1)
    rows_below = from_behind(page_cells[:, :offset], "tile", -1)
    normed = layer_norm(
        jnp.concatenate([page_cells[:, offset:], rows_below], axis=1).astype(jnp.float32)
    ).astype(jnp.bfloat16)
    projected = jnp.einsum(
        "prcd,de->prce", normed, joined, preferred_element_type=jnp.float32
    ).astype(jnp.bfloat16)
    projected = jnp.roll(projected, -offset, axis=2)
    per_row = columns // window
    shaped = projected.reshape(pages_here, window, per_row, window, 3, heads_enc, HEAD_ENC)
    shaped = jnp.swapaxes(shaped, 1, 2).reshape(
        pages_here, per_row, window * window, 3, heads_enc, HEAD_ENC
    )
    win_q = shaped[:, :, :, 0]
    win_k = shaped[:, :, :, 1]
    win_v = shaped[:, :, :, 2]
    is_last = lax.axis_index("tile") == lax.axis_size("tile") - 1
    local_rows = jnp.arange(window, dtype=jnp.int32)
    row_region = jnp.where(is_last, jnp.where(local_rows < window - offset, 1, 2), 0).astype(
        jnp.int32
    )
    labels = row_region[:, None] * 3 + regions(columns, window, offset)[None, :]
    labels = jnp.swapaxes(labels.reshape(window, per_row, window), 0, 1).reshape(
        per_row, window * window
    )
    allowed = labels[:, :, None] == labels[:, None, :]
    win_scores = jnp.einsum(
        "pnqhd,pnkhd->pnhqk", win_q, win_k, preferred_element_type=jnp.float32
    ) / math.sqrt(HEAD_ENC)
    win_scores = jnp.where(allowed[None, :, None], win_scores, -jnp.inf)
    top = jnp.max(win_scores, axis=-1, keepdims=True)
    expd = jnp.exp(win_scores - top)
    win_weights = (expd / jnp.sum(expd, axis=-1, keepdims=True)).astype(jnp.bfloat16)
    win_out = jnp.einsum(
        "pnhqk,pnkhd->pnqhd", win_weights, win_v, preferred_element_type=jnp.float32
    ).astype(jnp.bfloat16)
    win_out = win_out.reshape(pages_here, per_row, window, window, hq_enc)
    win_out = jnp.swapaxes(win_out, 1, 2).reshape(pages_here, window, columns, hq_enc)
    win_out = jnp.roll(win_out, offset, axis=2)
    rows_above = from_behind(win_out[:, window - offset :], "tile", 1)
    unrolled = jnp.concatenate([rows_above, win_out[:, : window - offset]], axis=1)
    partial_proj = jnp.einsum(
        "prce,ed->prcd", unrolled, wproj_enc, preferred_element_type=jnp.float32
    )
    summed = lax.psum(partial_proj.astype(jnp.bfloat16), "mp").astype(jnp.float32)
    encoded = (page_cells.astype(jnp.float32) + summed).astype(jnp.bfloat16)
    hq_dec = wq_dec.shape[1]
    heads_dec = hq_dec // HEAD_DEC
    page_normed = (
        layer_norm(encoded.astype(jnp.float32))
        .astype(jnp.bfloat16)
        .reshape(pages_here, own_rows, width)
    )
    page_kv = jnp.einsum(
        "pnd,de->pne",
        page_normed,
        wkv_dec.reshape(width, 2 * hq_dec),
        preferred_element_type=jnp.float32,
    ).astype(jnp.bfloat16)
    text_normed = layer_norm(text_states.astype(jnp.float32)).astype(jnp.bfloat16)
    queries = jnp.einsum(
        "ptd,de->pte", text_normed, wq_dec, preferred_element_type=jnp.float32
    ).astype(jnp.bfloat16)
    text_len = text_states.shape[1]
    query_heads = queries.reshape(pages_here, text_len, heads_dec, HEAD_DEC)
    start_state = (
        jnp.full((pages_here, heads_dec, text_len), -jnp.inf, jnp.float32),
        jnp.zeros((pages_here, heads_dec, text_len), jnp.float32),
        jnp.zeros((pages_here, heads_dec, text_len, HEAD_DEC), jnp.float32),
    )
    carried = start_state
    shard_rows = lax.all_gather(page_kv, "tile", axis=1, tiled=True)
    count = shard_rows.shape[1] // own_rows
    grouped = max(
        (
            factor
            for factor in range(1, count + 1)
            if count % factor == 0 and factor * own_rows <= 2048
        )
    )
    blocks = jnp.moveaxis(
        shard_rows.reshape(pages_here, count // grouped, grouped * own_rows, 2 * hq_dec), 1, 0
    )

    def advance(running, block_kv):
        maxima, totals, accum = running
        span = block_kv.shape[1]
        block_keys = block_kv[..., :hq_dec].reshape(pages_here, span, heads_dec, HEAD_DEC)
        block_vals = block_kv[..., hq_dec:].reshape(pages_here, span, heads_dec, HEAD_DEC)
        cross_scores = jnp.einsum(
            "pqhd,pkhd->phqk", query_heads, block_keys, preferred_element_type=jnp.float32
        ) / math.sqrt(HEAD_DEC)
        newest = jnp.maximum(maxima, jnp.max(cross_scores, axis=-1))
        rescale = jnp.exp(maxima - newest)
        expo = jnp.exp(cross_scores - newest[..., None])
        totals = totals * rescale + jnp.sum(expo, axis=-1)
        accum = accum * rescale[..., None] + jnp.einsum(
            "phqk,pkhd->phqd",
            expo.astype(jnp.bfloat16),
            block_vals,
            preferred_element_type=jnp.float32,
        )
        return ((newest, totals, accum), None)

    carried, unused = lax.scan(advance, carried, blocks)
    maxima, totals, accum = carried
    context = (
        jnp.transpose(accum / totals[..., None], (0, 2, 1, 3))
        .reshape(pages_here, text_len, hq_dec)
        .astype(jnp.bfloat16)
    )
    share = text_len // lax.axis_size("mp")
    mixed = lax.psum_scatter(
        jnp.einsum("pte,ed->tpd", context, wout_dec, preferred_element_type=jnp.float32).astype(
            jnp.bfloat16
        ),
        "mp",
        scatter_dimension=0,
        tiled=True,
    ).astype(jnp.float32)
    own_text = lax.dynamic_slice_in_dim(text_states, lax.axis_index("mp") * share, share, 1)
    decoded = (own_text.astype(jnp.float32) + jnp.moveaxis(mixed, 0, 1)).astype(jnp.bfloat16)
    return (encoded, decoded)


def solution(mesh):
    placed = (
        P(("pages", "batch"), "tile", None, None),
        P(("pages", "batch"), "tile", None),
        P("batch", "mp"),
        P("batch", None, "mp"),
        P("mp", "batch"),
        P("batch", "mp"),
        P("batch", None, "mp"),
        P("mp", "batch"),
    )
    return jax.shard_map(
        body,
        mesh=mesh,
        in_specs=placed,
        out_specs=(
            P(("pages", "batch"), "tile", None, None),
            P(("pages", "batch"), ("tile", "mp"), None),
        ),
        check_vma=False,
    )
```

profile of v0, /device:TPU:0, one launch (start us, length us, event | category | flops | bytes accessed | tf_op | source)
XLA Modules:
  0.0 199.5 jit_solution(16749749369688853707)
XLA Ops:
  9.6 5.1 %collective-permute-start = (bf16[1,6,24,1024]{3,2,1,0:T(8,128)(2,1)S(1)}, bf16[1,6,24,1024]{3,2,1,0:T(8,128)(2,1)S(1)}, u32[]{:S(2)}, u32[]{:S(2)}) collective-permute-start(bf16[1,6,24,1024]{3,2,1,0:T(8,128)(2,1)S(1)} %get-tuple-element.29), channel_id=1, source_target_pairs={{0,12},{4,0},{8,4},{12,8},{1,13},{5,1},{9,5},{13,9},{2,14},{6,2},{... | collective-permute-start | bytes 884744 | tf_op jit(solution)/shard_map/ppermute | solution.py:13
  15.8 5.1 %collective-permute-done = bf16[1,6,24,1024]{3,2,1,0:T(8,128)(2,1)S(1)} collective-permute-done((bf16[1,6,24,1024]{3,2,1,0:T(8,128)(2,1)S(1)}, bf16[1,6,24,1024]{3,2,1,0:T(8,128)(2,1)S(1)}, u32[]{:S(2)}, u32[]{:S(2)}) %collective-permute-start) | collective-permute-done | bytes 294944 | tf_op jit(solution)/shard_map/ppermute | solution.py:13
  21.4 1.5 all-gather.11.cloned.1.call-done
  22.9 2.1 %copy.40 = bf16[128,8,2,512]{3,1,2,0:T(8,128)(2,1)S(1)} copy(bf16[128,8,2,512]{3,2,1,0:T(2,128)(2,1)} %bitcast.102) | data formatting | bytes 4194304
  25.1 9.6 %all-gather.9.cloned.1.call-done = bf16[1024,512]{1,0:T(8,128)(2,1)} async-done(((bf16[512,512]{1,0:T(8,128)(2,1)}), bf16[1024,512]{1,0:T(8,128)(2,1)}) %all-gather.9.cloned.1.call-update) | async-done | bytes 1048592 | tf_op jit(solution)/shard_map/all_gather | solution.py:31
  34.7 2.4 %fusion.12 = bf16[1,12,24,1536]{3,2,1,0:T(8,128)(2,1)S(1)} fusion(bf16[1024,1024]{1,0:T(8,128)(2,1)S(1)} %bitcast.104, bf16[1024,512]{1,0:T(8,128)(2,1)} %all-gather.9.cloned.1.call-done, bf16[6,24,1024]{2,1,0:T(8,128)(2,1)S(1)} %bitcast.106, bf16[6,24,1024]{2,1,0:T(8,128)(2,1)S(1)} %get-tuple-element.28, f32[12,24]{1,0:T(8,128)S(1)} %add_sqrt_fusion.1, ...), kind=kOutput, calls=%fused_computation.17 | convolution fusion | flops 914178048 | bytes 4622592 | tf_op jit(solution)/shard_map/prcd,de->prce/dot_general | solution.py:48
  37.4 1.1 pad_maximum_fusion
  38.5 3.7 %reshape.311 = bf16[1,12,2,12,3,16,32]{6,5,4,3,2,1,0:T(8,128)(2,1)S(1)} reshape(bf16[1,12,24,1536]{3,2,1,0:T(8,128)(2,1)} %pad_maximum_fusion) | data formatting | bytes 1769472 | tf_op jit(solution)/shard_map/reshape | solution.py:53
  43.4 1.7 copy.39
  45.1 1.0 copy.38
  46.2 1.0 copy.37
  47.2 4.0 %fusion.81 = (f32[2,16,144]{2,1,0:T(8,128)S(1)}, f32[2,16,144,144]{2,3,1,0:T(8,128)}) fusion(pred[2,144,144]{1,2,0:T(8,128)(4,1)S(1)} %copy-done.8, bf16[1,2,144,1,16,32]{2,5,4,1,3,0:T(8,128)(2,1)S(1)} %copy-done.7, bf16[1,2,144,1,16,32]{2,5,4,1,3,0:T(8,128)(2,1)S(1)} %copy.38), kind=kOutput, calls=%fused_computation.103 | convolution fusion | flops 45121680 | bytes 3303936 | tf_op jit(solution)/shard_map/sub | solution.py:75
  51.2 2.8 %fusion.23 = bf16[1,2,144,16,32]{2,4,3,1,0:T(8,128)(2,1)S(1)} fusion(f32[2,16,144,144]{2,3,1,0:T(8,128)} %get-tuple-element.33, f32[2,16,144]{2,1,0:T(8,128)S(1)} %get-tuple-element.32, bf16[1,2,144,1,16,32]{2,5,4,1,3,0:T(8,128)(2,1)S(1)} %copy.37), kind=kOutput, calls=%fused_computation.37 | convolution fusion | flops 43941888 | bytes 3262464 | tf_op jit(solution)/shard_map/pnhqk,pnkhd->pnqhd/dot_general | solution.py:77
  54.0 1.1 copy.31
  56.2 1.8 collective-permute-start.1
  58.0 6.2 %collective-permute-done.1 = bf16[1,6,24,512]{3,2,1,0:T(8,128)(2,1)S(1)} collective-permute-done((bf16[1,6,24,512]{3,2,1,0:T(8,128)(2,1)S(1)}, bf16[1,6,24,512]{3,2,1,0:T(8,128)(2,1)S(1)}, u32[]{:S(2)}, u32[]{:S(2)}) %collective-permute-start.1) | collective-permute-done | bytes 147488 | tf_op jit(solution)/shard_map/ppermute | solution.py:13
  64.1 2.5 %fusion.20 = bf16[1,12,24,1024]{3,2,1,0:T(8,128)(2,1)} fusion(bf16[512,1024]{1,0:T(8,128)(2,1)} %all-gather.13.cloned.1.call-done, bf16[1,12,18,512]{3,2,1,0:T(8,128)(2,1)S(1)} %bitcast.99, bf16[1,12,6,512]{3,2,1,0:T(8,128)(2,1)S(1)} %slice.63, bf16[1,6,24,512]{3,2,1,0:T(8,128)(2,1)S(1)} %collective-permute-done.1), kind=kOutput, calls=%fused_computation.34 | convolution fusion | flops 303169536 | bytes 2080768 | tf_op jit(solution)/shard_map/prce,ed->prcd/dot_general | solution.py:85
  67.5 3.6 %copy.41 = bf16[128,8,2,512]{3,1,2,0:T(8,128)(2,1)} copy(bf16[128,8,2,512]{3,2,1,0:T(2,128)(2,1)} %bitcast.101) | data formatting | bytes 4194304
  71.1 25.1 %all-reduce.2.cloned.1.call-done = bf16[1,12,24,1024]{3,2,1,0:T(8,128)(2,1)} async-done(((bf16[1,12,24,1024]{3,2,1,0:T(8,128)(2,1)}), bf16[1,12,24,1024]{3,2,1,0:T(8,128)(2,1)}) %all-reduce.2.cloned.1.call-update) | async-done | bytes 589840 | tf_op jit(solution)/shard_map/psum | solution.py:88
  96.2 1.5 convert_reduce_fusion
  98.3 1.6 convolution_convert_fusion
  101.1 5.6 %all-gather.15.cloned.1.call-done = bf16[1024,512]{1,0:T(8,128)(2,1)} async-done(((bf16[512,512]{1,0:T(8,128)(2,1)}), bf16[1024,512]{1,0:T(8,128)(2,1)}) %all-gather.15.cloned.1.call-update) | async-done | bytes 1048592 | tf_op jit(solution)/shard_map/all_gather | solution.py:34
  106.8 1.7 convolution_convert_fusion.3
  109.3 50.8 %all-gather.21.cloned.1.call-done = bf16[1152,1024]{1,0:T(8,128)(2,1)} async-done(((bf16[288,1024]{1,0:T(8,128)(2,1)}), bf16[1152,1024]{1,0:T(8,128)(2,1)}) %all-gather.21.cloned.1.call-update) | async-done | bytes 2359312 | tf_op jit(solution)/shard_map/all_gather | solution.py:115
  160.1 1.8 fusion.79
  162.6 2.5 %multiply_reduce_fusion = (f32[8,256]{1,0:T(8,128)S(1)}, f32[8,256,1152]{2,1,0:T(8,128)S(1)}) fusion(bf16[256,8,64]{0,2,1:T(8,128)(2,1)} %bitcast.108, bf16[1152,8,64]{0,2,1:T(8,128)(2,1)S(1)} %bitcast.97), kind=kOutput, calls=%fused_computation.2 | convolution fusion | flops 306706432 | bytes 10887168 | tf_op jit(solution)/shard_map/while/body/eval_jaxpr/pqhd,pkhd->phqk/dot_general | solution.py:133
  165.1 1.9 fusion.1
  167.0 1.7 copy-done
  169.4 5.5 %fusion.40 = bf16[8,256,64]{1,2,0:T(8,128)(2,1)S(1)} fusion(bf16[1152,8,64]{0,2,1:T(8,128)(2,1)S(1)} %bitcast.105, f32[8,256,1152]{2,1,0:T(8,128)} %copy-done, f32[8,256]{1,0:T(8,128)S(1)} %get-tuple-element.34, f32[8,256]{1,0:T(8,128)S(1)} %get-tuple-element.31, f32[8,256]{1,0:T(8,128)S(1)} %get-tuple-element.30), kind=kOutput, calls=%fused_computation.52 | convolution fusion | flops 309460992 | bytes 10903552 | tf_op jit(solution)/shard_map/while/body/eval_jaxpr/phqk,pkhd->phqd/dot_general | solution.py:140
  175.0 2.5 %fusion.24 = bf16[256,1,1024]{2,0,1:T(8,128)(2,1)} fusion(bf16[256,512]{0,1:T(8,128)(2,1)S(1)} %bitcast.110, bf16[512,1024]{1,0:T(8,128)(2,1)} %all-gather.19.cloned.1.call-done), kind=kOutput, calls=%fused_computation.38 | convolution fusion | flops 268697600 | bytes 1835008 | tf_op jit(solution)/shard_map/pte,ed->tpd/dot_general | solution.py:157
  177.6 13.6 %reduce-scatter.2.cloned.1.call-done = bf16[128,1,1024]{2,0,1:T(8,128)(2,1)} async-done(((bf16[256,1,1024]{2,0,1:T(8,128)(2,1)}), bf16[128,1,1024]{2,0,1:T(8,128)(2,1)}) %reduce-scatter.2.cloned.1.call-update) | async-done | bytes 262160 | tf_op jit(solution)/shard_map/reduce_scatter | solution.py:156
  191.2 1.7 fusion.50
  (72 shorter events, 11.3 us)
Async XLA Ops:
  7.2 2.3 %copy-start.4 = (bf16[1,12,24,1024]{3,2,1,0:T(8,128)(2,1)S(1)}, bf16[1,12,24,1024]{3,2,1,0:T(8,128)(2,1)}, u32[]{:S(2)}) copy-start(bf16[1,12,24,1024]{3,2,1,0:T(8,128)(2,1)} %param.8) | copy-start | bytes 1769476
  7.2 15.8 %all-gather.11.cloned.1.call-start = ((), (), s32[]{:S(2)}) async-start(), calls=%async_computation.2 | async-start | bytes 3145728 | tf_op jit(solution)/shard_map/all_gather | solution.py:32
  7.9 26.8 %all-gather.9.cloned.1.call-start = ((), (), s32[]{:S(2)}) async-start(), calls=%async_computation.1 | async-start | bytes 1572864 | tf_op jit(solution)/shard_map/all_gather | solution.py:31
  8.7 49.3 %all-gather.13.cloned.1.call-start = ((), (), s32[]{:S(2)}) async-start(), calls=%async_computation.3 | async-start | bytes 1572864 | tf_op jit(solution)/shard_map/all_gather | solution.py:33
  9.4 58.1 %all-gather.17.cloned.1.call-start = ((), (), s32[]{:S(2)}) async-start(), calls=%async_computation.6 | async-start | bytes 3145728 | tf_op jit(solution)/shard_map/all_gather | solution.py:35
  9.6 11.4 %collective-permute-start = (bf16[1,6,24,1024]{3,2,1,0:T(8,128)(2,1)S(1)}, bf16[1,6,24,1024]{3,2,1,0:T(8,128)(2,1)S(1)}, u32[]{:S(2)}, u32[]{:S(2)}) collective-permute-start(bf16[1,6,24,1024]{3,2,1,0:T(8,128)(2,1)S(1)} %get-tuple-element.29), channel_id=1, source_target_pairs={{0,12},{4,0},{8,4},{12,8},{1,13},{5,1},{9,5},{13,9},{2,14},{6,2},{... | collective-permute-start | bytes 884744 | tf_op jit(solution)/shard_map/ppermute | solution.py:13
  14.7 81.5 %all-reduce.2.cloned.1.call-start = ((), (), s32[]{:S(2)}) async-start(), calls=%async_computation.4 | async-start | bytes 1179648 | tf_op jit(solution)/shard_map/psum | solution.py:88
  45.1 2.1 %copy-start.7 = (bf16[1,2,144,1,16,32]{2,5,4,1,3,0:T(8,128)(2,1)S(1)}, bf16[1,2,144,1,16,32]{2,5,4,1,3,0:T(8,128)(2,1)}, u32[]{:S(2)}) copy-start(bf16[1,2,144,1,16,32]{2,5,4,1,3,0:T(8,128)(2,1)} %copy.39) | copy-start | bytes 884740
  45.1 2.1 %copy-start.8 = (pred[2,144,144]{1,2,0:T(8,128)(4,1)S(1)}, pred[2,144,144]{1,2,0:T(8,128)(4,1)}, u32[]{:S(2)}) copy-start(pred[2,144,144]{1,2,0:T(8,128)(4,1)} %broadcast_compare_fusion) | copy-start | bytes 124420
  56.2 8.0 %collective-permute-start.1 = (bf16[1,6,24,512]{3,2,1,0:T(8,128)(2,1)S(1)}, bf16[1,6,24,512]{3,2,1,0:T(8,128)(2,1)S(1)}, u32[]{:S(2)}, u32[]{:S(2)}) collective-permute-start(bf16[1,6,24,512]{3,2,1,0:T(8,128)(2,1)S(1)} %fusion.70), channel_id=1, source_target_pairs={{0,4},{4,8},{8,12},{12,0},{1,5},{5,9},{9,13},{13,1},{2,6},{6,10},{... | collective-permute-start | bytes 442376 | tf_op jit(solution)/shard_map/ppermute | solution.py:13
  66.7 40.1 %all-gather.15.cloned.1.call-start = ((), (), s32[]{:S(2)}) async-start(), calls=%async_computation.5 | async-start | bytes 1572864 | tf_op jit(solution)/shard_map/all_gather | solution.py:34
  67.3 92.8 %all-gather.21.cloned.1.call-start = ((), (), s32[]{:S(2)}) async-start(), calls=%async_computation.9 | async-start | bytes 2949120 | tf_op jit(solution)/shard_map/all_gather | solution.py:115
  67.5 28.7 %copy-start.5 = (bf16[1,12,24,1024]{3,2,1,0:T(8,128)(2,1)S(1)}, bf16[1,12,24,1024]{3,2,1,0:T(8,128)(2,1)}, u32[]{:S(2)}) copy-start(bf16[1,12,24,1024]{3,2,1,0:T(8,128)(2,1)} %param.8) | copy-start | bytes 1769476
  96.2 2.0 %copy-start.6 = (bf16[128,8,2,512]{3,1,2,0:T(8,128)(2,1)S(1)}, bf16[128,8,2,512]{3,1,2,0:T(8,128)(2,1)}, u32[]{:S(2)}) copy-start(bf16[128,8,2,512]{3,1,2,0:T(8,128)(2,1)} %copy.41) | copy-start | bytes 6291460
  97.7 2.2 %copy-start.1 = (bf16[1,12,24,1024]{3,2,1,0:T(8,128)(2,1)}, bf16[1,12,24,1024]{3,2,1,0:T(8,128)(2,1)S(1)}, u32[]{:S(2)}) copy-start(bf16[1,12,24,1024]{3,2,1,0:T(8,128)(2,1)S(1)} %get-tuple-element.15) | copy-start | bytes 1769476
  98.2 2.4 %copy-start.2 = (bf16[1,256,1024]{2,1,0:T(8,128)(2,1)S(1)}, bf16[1,256,1024]{2,1,0:T(8,128)(2,1)}, u32[]{:S(2)}) copy-start(bf16[1,256,1024]{2,1,0:T(8,128)(2,1)} %param.9) | copy-start | bytes 1572868
  99.9 75.1 %all-gather.19.cloned.1.call-start = ((), (), s32[]{:S(2)}) async-start(), calls=%async_computation.7 | async-start | bytes 1572864 | tf_op jit(solution)/shard_map/all_gather | solution.py:36
  100.6 90.6 %reduce-scatter.2.cloned.1.call-start = ((), (), s32[]{:S(2)}) async-start(), calls=%async_computation.8 | async-start | bytes 786432 | tf_op jit(solution)/shard_map/reduce_scatter | solution.py:156
  165.1 3.7 %copy-start = (f32[8,256,1152]{2,1,0:T(8,128)}, f32[8,256,1152]{2,1,0:T(8,128)S(1)}, u32[]{:S(2)}) copy-start(f32[8,256,1152]{2,1,0:T(8,128)S(1)} %get-tuple-element.35) | copy-start | bytes 28311556
  175.0 16.3 %copy-start.3 = (bf16[1,256,1024]{2,1,0:T(8,128)(2,1)S(1)}, bf16[1,256,1024]{2,1,0:T(8,128)(2,1)}, u32[]{:S(2)}) copy-start(bf16[1,256,1024]{2,1,0:T(8,128)(2,1)} %param.9) | copy-start | bytes 1572868
Sparse Core Ops, SparseCore 0:
  9.6 13.3 all-gather.10
  24.5 10.1 all-gather.8
  36.3 10.1 all-gather.12
  47.9 11.7 all-gather.16
  66.8 29.3 all-reduce.1
  97.7 9.0 all-gather.14
  108.4 51.6 all-gather.20
  161.7 7.8 all-gather.18
  177.7 13.4 reduce-scatter.1
where the time goes:
time: 200 us; the launch traced here: 199 us
  waiting for transfers between devices  121 us (60%)
  matrix products  25.6 us (13%)
  local copies, waits for them, and re-layouts  22.9 us (11%)
  between operations  14.2 us (7%)
  other arithmetic  8.42 us (4%)
  starting transfers between devices  7.43 us (4%)
    all_gather x1, waiting for transfers between devices, body(): shard_rows = lax.all_gather(page_kv, 'tile', axis=1, tiled=True)  50.8 us
    psum x1, waiting for transfers between devices, body(): lax.psum(partial_proj.astype(jnp.bfloat16), 'mp').astype(jnp.float32)  25.1 us
    reduce_scatter x1, waiting for transfers between devices, body(): lax.psum_scatter(jnp.einsum('pte,ed->tpd', context, wout_dec, preferred_e...  13.6 us
    ppermute x2, waiting for transfers between devices, from_behind(): lax.ppermute(value, axis, [(i, (i + by) % devices) for i in range(devices)])  11.3 us
    unnamed x23, local copies, waits for them, and re-layouts  11.3 us
    all_gather x1, waiting for transfers between devices, body(): lax.all_gather(enc_query, 'batch', axis=0, tiled=True)  9.63 us
    ppermute x2, starting transfers between devices, from_behind(): lax.ppermute(value, axis, [(i, (i + by) % devices) for i in range(devices)])  6.9 us
    all_gather x1, waiting for transfers between devices, body(): lax.all_gather(dec_query, 'batch', axis=0, tiled=True)  5.6 us
  transfers between devices with their start and end apart: 11, of which 8 were waited for; matrix products, arithmetic and copies ran while one was open for 25% of the time, Pallas kernels for 0%

commit v1 on v0

--- a/solution.py
+++ b/solution.py
@@ -6,6 +6,11 @@
 
 HEAD_ENC = 32
 HEAD_DEC = 64
+
+
+def gather_and_add(array, axis):
+    blocks = lax.all_gather(array, axis)
+    return jnp.sum(blocks, axis=0)
 
 
 def from_behind(value, axis, by):
@@ -85,7 +90,7 @@
     partial_proj = jnp.einsum(
         "prce,ed->prcd", unrolled, wproj_enc, preferred_element_type=jnp.float32
     )
-    summed = lax.psum(partial_proj.astype(jnp.bfloat16), "mp").astype(jnp.float32)
+    summed = gather_and_add(partial_proj.astype(jnp.bfloat16), "mp").astype(jnp.float32)
     encoded = (page_cells.astype(jnp.float32) + summed).astype(jnp.bfloat16)
     hq_dec = wq_dec.shape[1]
     heads_dec = hq_dec // HEAD_DEC

time: 200 us -> 193 us (0.965)
  waiting for transfers between devices: 121 us -> 112 us
    psum x1 -> x0, waiting for transfers between devices: 25.1 us -> none  [body(): lax.psum(partial_proj.astype(jnp.bfloat16), 'mp').astype(jnp.float32)]
    all_gather x0 -> x1, waiting for transfers between devices: none -> 17.8 us  [gather_and_add(): blocks = lax.all_gather(array, axis)]
  transfers between devices with their start and end apart: 11 -> 11, of which waited for: 8 -> 8; matrix products, arithmetic and copies ran while one was open for 25% -> 27% of each run, Pallas kernels for 0% -> 0%
where the time goes in v1:
time: 193 us; the launch traced here: 192 us
  waiting for transfers between devices  112 us (58%)
  matrix products  25.6 us (13%)
  local copies, waits for them, and re-layouts  23.9 us (12%)
  between operations  14.2 us (7%)
  other arithmetic  8.77 us (5%)
  starting transfers between devices  7.43 us (4%)
    all_gather x1, waiting for transfers between devices, body(): shard_rows = lax.all_gather(page_kv, 'tile', axis=1, tiled=True)  50.7 us
    all_gather x1, waiting for transfers between devices, gather_and_add(): blocks = lax.all_gather(array, axis)  17.8 us
    reduce_scatter x1, waiting for transfers between devices, body(): lax.psum_scatter(jnp.einsum('pte,ed->tpd', context, wout_dec, preferred_e...  13.6 us
    unnamed x23, local copies, waits for them, and re-layouts  12.3 us
    ppermute x2, waiting for transfers between devices, from_behind(): lax.ppermute(value, axis, [(i, (i + by) % devices) for i in range(devices)])  11.3 us
    all_gather x1, waiting for transfers between devices, body(): lax.all_gather(enc_query, 'batch', axis=0, tiled=True)  9.63 us
    ppermute x2, starting transfers between devices, from_behind(): lax.ppermute(value, axis, [(i, (i + by) % devices) for i in range(devices)])  6.9 us
    dot_general x1, matrix products, advance(): jnp.einsum('phqk,pkhd->phqd', expo.astype(jnp.bfloat16), block_vals, pref...  5.51 us
  transfers between devices with their start and end apart: 11, of which 8 were waited for; matrix products, arithmetic and copies ran while one was open for 27% of the time, Pallas kernels for 0%

profile of v1, /device:TPU:0, one launch (start us, length us, event | category | flops | bytes accessed | tf_op | source)
XLA Modules:
  0.0 192.1 jit_solution(4294889195947293891)
XLA Ops:
  9.6 5.1 %collective-permute-start = (bf16[1,6,24,1024]{3,2,1,0:T(8,128)(2,1)S(1)}, bf16[1,6,24,1024]{3,2,1,0:T(8,128)(2,1)S(1)}, u32[]{:S(2)}, u32[]{:S(2)}) collective-permute-start(bf16[1,6,24,1024]{3,2,1,0:T(8,128)(2,1)S(1)} %get-tuple-element.29), channel_id=1, source_target_pairs={{0,12},{4,0},{8,4},{12,8},{1,13},{5,1},{9,5},{13,9},{2,14},{6,2},{... | collective-permute-start | bytes 884744 | tf_op jit(solution)/shard_map/ppermute | solution.py:18
  15.8 5.1 %collective-permute-done = bf16[1,6,24,1024]{3,2,1,0:T(8,128)(2,1)S(1)} collective-permute-done((bf16[1,6,24,1024]{3,2,1,0:T(8,128)(2,1)S(1)}, bf16[1,6,24,1024]{3,2,1,0:T(8,128)(2,1)S(1)}, u32[]{:S(2)}, u32[]{:S(2)}) %collective-permute-start) | collective-permute-done | bytes 294944 | tf_op jit(solution)/shard_map/ppermute | solution.py:18
  21.4 1.5 all-gather.13.cloned.1.call-done
  22.9 2.1 %copy.40 = bf16[128,8,2,512]{3,1,2,0:T(8,128)(2,1)S(1)} copy(bf16[128,8,2,512]{3,2,1,0:T(2,128)(2,1)} %bitcast.103) | data formatting | bytes 4194304
  25.1 9.6 %all-gather.11.cloned.1.call-done = bf16[1024,512]{1,0:T(8,128)(2,1)} async-done(((bf16[512,512]{1,0:T(8,128)(2,1)}), bf16[1024,512]{1,0:T(8,128)(2,1)}) %all-gather.11.cloned.1.call-update) | async-done | bytes 1048592 | tf_op jit(solution)/shard_map/all_gather | solution.py:36
  34.7 2.4 %fusion.12 = bf16[1,12,24,1536]{3,2,1,0:T(8,128)(2,1)S(1)} fusion(bf16[1024,1024]{1,0:T(8,128)(2,1)S(1)} %bitcast.105, bf16[1024,512]{1,0:T(8,128)(2,1)} %all-gather.11.cloned.1.call-done, bf16[6,24,1024]{2,1,0:T(8,128)(2,1)S(1)} %bitcast.110, bf16[6,24,1024]{2,1,0:T(8,128)(2,1)S(1)} %get-tuple-element.28, f32[12,24]{1,0:T(8,128)S(1)} %add_sqrt_fusion.1, ...), kind=kOutput, calls=%fused_computation.17 | convolution fusion | flops 914178048 | bytes 4622592 | tf_op jit(solution)/shard_map/prcd,de->prce/dot_general | solution.py:53
  37.4 1.1 pad_maximum_fusion
  38.5 3.7 %reshape.323 = bf16[1,12,2,12,3,16,32]{6,5,4,3,2,1,0:T(8,128)(2,1)S(1)} reshape(bf16[1,12,24,1536]{3,2,1,0:T(8,128)(2,1)} %pad_maximum_fusion) | data formatting | bytes 1769472 | tf_op jit(solution)/shard_map/reshape | solution.py:58
  43.4 1.7 copy.39
  45.1 1.0 copy.38
  46.2 1.0 copy.37
  47.2 4.0 %fusion.82 = (f32[2,16,144]{2,1,0:T(8,128)S(1)}, f32[2,16,144,144]{2,3,1,0:T(8,128)}) fusion(pred[2,144,144]{1,2,0:T(8,128)(4,1)S(1)} %copy-done.8, bf16[1,2,144,1,16,32]{2,5,4,1,3,0:T(8,128)(2,1)S(1)} %copy-done.7, bf16[1,2,144,1,16,32]{2,5,4,1,3,0:T(8,128)(2,1)S(1)} %copy.38), kind=kOutput, calls=%fused_computation.103 | convolution fusion | flops 45121680 | bytes 3303936 | tf_op jit(solution)/shard_map/sub | solution.py:80
  51.2 2.8 %fusion.22 = bf16[1,2,144,16,32]{2,4,3,1,0:T(8,128)(2,1)S(1)} fusion(f32[2,16,144,144]{2,3,1,0:T(8,128)} %get-tuple-element.33, f32[2,16,144]{2,1,0:T(8,128)S(1)} %get-tuple-element.32, bf16[1,2,144,1,16,32]{2,5,4,1,3,0:T(8,128)(2,1)S(1)} %copy.37), kind=kOutput, calls=%fused_computation.36 | convolution fusion | flops 43941888 | bytes 3262464 | tf_op jit(solution)/shard_map/pnhqk,pnkhd->pnqhd/dot_general | solution.py:82
  54.0 1.1 copy.31
  56.2 1.8 collective-permute-start.1
  58.0 6.2 %collective-permute-done.1 = bf16[1,6,24,512]{3,2,1,0:T(8,128)(2,1)S(1)} collective-permute-done((bf16[1,6,24,512]{3,2,1,0:T(8,128)(2,1)S(1)}, bf16[1,6,24,512]{3,2,1,0:T(8,128)(2,1)S(1)}, u32[]{:S(2)}, u32[]{:S(2)}) %collective-permute-start.1) | collective-permute-done | bytes 147488 | tf_op jit(solution)/shard_map/ppermute | solution.py:18
  64.1 2.5 %convolution_convert_fusion.1 = bf16[12,24,1024]{2,1,0:T(8,128)(2,1)} fusion(bf16[512,1024]{1,0:T(8,128)(2,1)} %all-gather.15.cloned.1.call-done, bf16[1,12,18,512]{3,2,1,0:T(8,128)(2,1)S(1)} %bitcast.107, bf16[1,12,6,512]{3,2,1,0:T(8,128)(2,1)S(1)} %slice.63, bf16[1,6,24,512]{3,2,1,0:T(8,128)(2,1)S(1)} %collective-permute-done.1), kind=kOutput, calls=%fused_computation.29 | convolution fusion | flops 303169536 | bytes 2080768 | tf_op jit(solution)/shard_map/prce,ed->prcd/dot_general | solution.py:90
  67.5 3.6 %copy.41 = bf16[128,8,2,512]{3,1,2,0:T(8,128)(2,1)} copy(bf16[128,8,2,512]{3,2,1,0:T(2,128)(2,1)} %bitcast.102) | data formatting | bytes 4194304
  71.1 17.8 %all-gather.23.cloned.1.call-done = bf16[24,24,1024]{2,1,0:T(8,128)(2,1)} async-done(((bf16[12,24,1024]{2,1,0:T(8,128)(2,1)}), bf16[24,24,1024]{2,1,0:T(8,128)(2,1)}) %all-gather.23.cloned.1.call-update) | async-done | bytes 1179664 | tf_op jit(solution)/shard_map/all_gather | solution.py:12
  88.9 1.6 reduce.16
  92.3 1.6 convolution_convert_fusion
  95.2 4.2 %all-gather.17.cloned.1.call-done = bf16[1024,512]{1,0:T(8,128)(2,1)} async-done(((bf16[512,512]{1,0:T(8,128)(2,1)}), bf16[1024,512]{1,0:T(8,128)(2,1)}) %all-gather.17.cloned.1.call-update) | async-done | bytes 1048592 | tf_op jit(solution)/shard_map/all_gather | solution.py:39
  99.4 1.7 convolution_convert_fusion.3
  102.0 50.7 %all-gather.25.cloned.1.call-done = bf16[1152,1024]{1,0:T(8,128)(2,1)} async-done(((bf16[288,1024]{1,0:T(8,128)(2,1)}), bf16[1152,1024]{1,0:T(8,128)(2,1)}) %all-gather.25.cloned.1.call-update) | async-done | bytes 2359312 | tf_op jit(solution)/shard_map/all_gather | solution.py:120
  152.7 1.8 fusion.80
  155.2 2.5 %multiply_reduce_fusion = (f32[8,256]{1,0:T(8,128)S(1)}, f32[8,256,1152]{2,1,0:T(8,128)S(1)}) fusion(bf16[256,8,64]{0,2,1:T(8,128)(2,1)} %bitcast.112, bf16[1152,8,64]{0,2,1:T(8,128)(2,1)S(1)} %bitcast.100), kind=kOutput, calls=%fused_computation.2 | convolution fusion | flops 306706432 | bytes 10887168 | tf_op jit(solution)/shard_map/while/body/eval_jaxpr/pqhd,pkhd->phqk/dot_general | solution.py:138
  157.7 1.9 fusion.1
  159.6 1.7 copy-done
  162.0 5.5 %fusion.40 = bf16[8,256,64]{1,2,0:T(8,128)(2,1)S(1)} fusion(bf16[1152,8,64]{0,2,1:T(8,128)(2,1)S(1)} %bitcast.109, f32[8,256,1152]{2,1,0:T(8,128)} %copy-done, f32[8,256]{1,0:T(8,128)S(1)} %get-tuple-element.34, f32[8,256]{1,0:T(8,128)S(1)} %get-tuple-element.31, f32[8,256]{1,0:T(8,128)S(1)} %get-tuple-element.30), kind=kOutput, calls=%fused_computation.52 | convolution fusion | flops 309460992 | bytes 10903552 | tf_op jit(solution)/shard_map/while/body/eval_jaxpr/phqk,pkhd->phqd/dot_general | solution.py:145
  167.6 2.5 %fusion.23 = bf16[256,1,1024]{2,0,1:T(8,128)(2,1)} fusion(bf16[256,512]{0,1:T(8,128)(2,1)S(1)} %bitcast.114, bf16[512,1024]{1,0:T(8,128)(2,1)} %all-gather.21.cloned.1.call-done), kind=kOutput, calls=%fused_computation.37 | convolution fusion | flops 268697600 | bytes 1835008 | tf_op jit(solution)/shard_map/pte,ed->tpd/dot_general | solution.py:162
  170.2 13.6 %reduce-scatter.2.cloned.1.call-done = bf16[128,1,1024]{2,0,1:T(8,128)(2,1)} async-done(((bf16[256,1,1024]{2,0,1:T(8,128)(2,1)}), bf16[128,1,1024]{2,0,1:T(8,128)(2,1)}) %reduce-scatter.2.cloned.1.call-update) | async-done | bytes 262160 | tf_op jit(solution)/shard_map/reduce_scatter | solution.py:161
  183.8 1.7 fusion.50
  (73 shorter events, 12.5 us)
Async XLA Ops:
  7.2 2.3 %copy-start.4 = (bf16[1,12,24,1024]{3,2,1,0:T(8,128)(2,1)S(1)}, bf16[1,12,24,1024]{3,2,1,0:T(8,128)(2,1)}, u32[]{:S(2)}) copy-start(bf16[1,12,24,1024]{3,2,1,0:T(8,128)(2,1)} %param.8) | copy-start | bytes 1769476
  7.2 15.8 %all-gather.13.cloned.1.call-start = ((), (), s32[]{:S(2)}) async-start(), calls=%async_computation.2 | async-start | bytes 3145728 | tf_op jit(solution)/shard_map/all_gather | solution.py:37
  7.9 26.8 %all-gather.11.cloned.1.call-start = ((), (), s32[]{:S(2)}) async-start(), calls=%async_computation.1 | async-start | bytes 1572864 | tf_op jit(solution)/shard_map/all_gather | solution.py:36
  8.7 49.3 %all-gather.15.cloned.1.call-start = ((), (), s32[]{:S(2)}) async-start(), calls=%async_computation.3 | async-start | bytes 1572864 | tf_op jit(solution)/shard_map/all_gather | solution.py:38
  9.4 58.1 %all-gather.19.cloned.1.call-start = ((), (), s32[]{:S(2)}) async-start(), calls=%async_computation.5 | async-start | bytes 3145728 | tf_op jit(solution)/shard_map/all_gather | solution.py:40
  9.6 11.4 %collective-permute-start = (bf16[1,6,24,1024]{3,2,1,0:T(8,128)(2,1)S(1)}, bf16[1,6,24,1024]{3,2,1,0:T(8,128)(2,1)S(1)}, u32[]{:S(2)}, u32[]{:S(2)}) collective-permute-start(bf16[1,6,24,1024]{3,2,1,0:T(8,128)(2,1)S(1)} %get-tuple-element.29), channel_id=1, source_target_pairs={{0,12},{4,0},{8,4},{12,8},{1,13},{5,1},{9,5},{13,9},{2,14},{6,2},{... | collective-permute-start | bytes 884744 | tf_op jit(solution)/shard_map/ppermute | solution.py:18
  14.7 74.3 %all-gather.23.cloned.1.call-start = ((), (), s32[]{:S(2)}) async-start(), calls=%async_computation.8 | async-start | bytes 1769472 | tf_op jit(solution)/shard_map/all_gather | solution.py:12
  45.1 2.1 %copy-start.7 = (bf16[1,2,144,1,16,32]{2,5,4,1,3,0:T(8,128)(2,1)S(1)}, bf16[1,2,144,1,16,32]{2,5,4,1,3,0:T(8,128)(2,1)}, u32[]{:S(2)}) copy-start(bf16[1,2,144,1,16,32]{2,5,4,1,3,0:T(8,128)(2,1)} %copy.39) | copy-start | bytes 884740
  45.1 2.1 %copy-start.8 = (pred[2,144,144]{1,2,0:T(8,128)(4,1)S(1)}, pred[2,144,144]{1,2,0:T(8,128)(4,1)}, u32[]{:S(2)}) copy-start(pred[2,144,144]{1,2,0:T(8,128)(4,1)} %broadcast_compare_fusion) | copy-start | bytes 124420
  56.2 8.0 %collective-permute-start.1 = (bf16[1,6,24,512]{3,2,1,0:T(8,128)(2,1)S(1)}, bf16[1,6,24,512]{3,2,1,0:T(8,128)(2,1)S(1)}, u32[]{:S(2)}, u32[]{:S(2)}) collective-permute-start(bf16[1,6,24,512]{3,2,1,0:T(8,128)(2,1)S(1)} %fusion.70), channel_id=1, source_target_pairs={{0,4},{4,8},{8,12},{12,0},{1,5},{5,9},{9,13},{13,1},{2,6},{6,10},{... | collective-permute-start | bytes 442376 | tf_op jit(solution)/shard_map/ppermute | solution.py:18
  66.7 32.7 %all-gather.17.cloned.1.call-start = ((), (), s32[]{:S(2)}) async-start(), calls=%async_computation.4 | async-start | bytes 1572864 | tf_op jit(solution)/shard_map/all_gather | solution.py:39
  67.3 85.4 %all-gather.25.cloned.1.call-start = ((), (), s32[]{:S(2)}) async-start(), calls=%async_computation.9 | async-start | bytes 2949120 | tf_op jit(solution)/shard_map/all_gather | solution.py:120
  67.5 23.0 %copy-start.5 = (bf16[1,12,24,1024]{3,2,1,0:T(8,128)(2,1)S(1)}, bf16[1,12,24,1024]{3,2,1,0:T(8,128)(2,1)}, u32[]{:S(2)}) copy-start(bf16[1,12,24,1024]{3,2,1,0:T(8,128)(2,1)} %param.8) | copy-start | bytes 1769476
  90.5 1.8 copy-start.6
  90.8 3.2 %copy-start.1 = (bf16[1,12,24,1024]{3,2,1,0:T(8,128)(2,1)}, bf16[1,12,24,1024]{3,2,1,0:T(8,128)(2,1)S(1)}, u32[]{:S(2)}) copy-start(bf16[1,12,24,1024]{3,2,1,0:T(8,128)(2,1)S(1)} %get-tuple-element.15) | copy-start | bytes 1769476
  92.3 2.4 %copy-start.2 = (bf16[1,256,1024]{2,1,0:T(8,128)(2,1)S(1)}, bf16[1,256,1024]{2,1,0:T(8,128)(2,1)}, u32[]{:S(2)}) copy-start(bf16[1,256,1024]{2,1,0:T(8,128)(2,1)} %param.9) | copy-start | bytes 1572868
  94.0 73.6 %all-gather.21.cloned.1.call-start = ((), (), s32[]{:S(2)}) async-start(), calls=%async_computation.6 | async-start | bytes 1572864 | tf_op jit(solution)/shard_map/all_gather | solution.py:41
  94.7 89.1 %reduce-scatter.2.cloned.1.call-start = ((), (), s32[]{:S(2)}) async-start(), calls=%async_computation.7 | async-start | bytes 786432 | tf_op jit(solution)/shard_map/reduce_scatter | solution.py:161
  157.7 3.7 %copy-start = (f32[8,256,1152]{2,1,0:T(8,128)}, f32[8,256,1152]{2,1,0:T(8,128)S(1)}, u32[]{:S(2)}) copy-start(f32[8,256,1152]{2,1,0:T(8,128)S(1)} %get-tuple-element.35) | copy-start | bytes 28311556
  167.6 16.3 %copy-start.3 = (bf16[1,256,1024]{2,1,0:T(8,128)(2,1)S(1)}, bf16[1,256,1024]{2,1,0:T(8,128)(2,1)}, u32[]{:S(2)}) copy-start(bf16[1,256,1024]{2,1,0:T(8,128)(2,1)} %param.9) | copy-start | bytes 1572868
Sparse Core Ops, SparseCore 0:
  9.6 13.3 all-gather.12
  24.5 10.1 all-gather.10
  36.3 10.1 all-gather.14
  47.9 11.7 all-gather.18
  66.8 22.0 all-gather.22
  90.3 9.0 all-gather.16
  101.0 51.6 all-gather.24
  154.2 7.8 all-gather.20
  170.3 13.4 reduce-scatter.1
